TPU v7x, 32 devices: a whole 2x2x4 slice. The times are simulated.
32 devices in a mesh: lon: 8 (over y, x, core), lat: 4 (over z).
Axes of the slice: x: 2, y: 2, z: 4, core: 2. Of those that a mesh axis runs over, the one named last changes fastest.
Arguments:
- gradient: float32 [137, 16, 1024], P(None, 'lat', 'lon'), may hold values from -60 to 60
- obs_weight: float32 [137, 16, 1024], P(None, 'lat', 'lon'), may hold values from 0.2 to 5
- half_width: int32 [16], P('lat'), may hold values from 8 to 32
- zonal_coef: float32 [16, 33], P('lat'), may hold values from 0.2 to 1
- mirror_map: int32 [1024], P('lon'), may hold values from 0 to 1023, as said below
- merid_coef: float32 [5], replicated, may hold values from 0.2 to 1
- vertical_map: float32 [137, 137], replicated, may hold values from -0.5 to 0.5
Outputs:
- increment: float32 [137, 16, 1024], P(None, 'lat', 'lon')
- residual: float32 [137, 16, 1024], P(None, 'lat', 'lon')
Inputs may be any that keep to these rules, and one draw needn't show every extreme that they name: mirror_map[mirror_map[i]] = i, and mirror_map[i] lies in the block of 128 longitudes whose block index differs from i // 128 by 4.
All inputs are finite; a program needn't handle non-finite values.
Results may differ from a plain program's by a relative error of at most 0.04.
Values sent between devices are 32-bit elements; how exact they have to be, the bound alone decides.
No kernel may reach another device: no remote copies, remote signals or barrier semaphores. Data moves between devices by JAX's collectives and lax.ppermute only.
A program may use at most 64 MiB of HBM per device.

v0:
```python
import jax
import jax.numpy as jnp
from jax import lax
from jax.sharding import PartitionSpec as P

OUTER = 2


def extended_2(block, sides, width, periodic):
    for axis, dim in sides:
        count = lax.axis_size(axis)
        forward = [(i, i + 1) for i in range(count - 1)]
        if periodic:
            forward.append((count - 1, 0))
        backward = [(target, source) for source, target in forward]
        low = lax.ppermute(
            lax.slice_in_dim(block, block.shape[dim] - width, None, axis=dim), axis, forward
        )
        high = lax.ppermute(lax.slice_in_dim(block, 0, width, axis=dim), axis, backward)
        block = jnp.concatenate([low, block, high], axis=dim)
    return block


def from_partner(value, axis, distance):
    return lax.ppermute(value, axis, [(i, i ^ 1 << distance) for i in range(lax.axis_size(axis))])


def zonal_weights(half_width, zonal_coef):
    tap_ids = jnp.arange(zonal_coef.shape[1], dtype=jnp.int32)
    kept = jnp.where(
        tap_ids[None, :] <= half_width[:, None], zonal_coef, jnp.zeros_like(zonal_coef)
    )
    scaling = jnp.sqrt(kept[:, 0] ** 2 + 2.0 * jnp.sum(kept[:, 1:] ** 2, axis=1))
    return kept / scaling[:, None]


def merid_weights(merid_coef):
    norm_value = jnp.sqrt(merid_coef[0] ** 2 + 2.0 * jnp.sum(merid_coef[1:] ** 2))
    return merid_coef / norm_value


def zonal_tables(weights, lon_dev):
    width = weights.shape[1] - 1
    positions = jnp.arange(lon_dev + 2 * width, dtype=jnp.int32)
    columns = jnp.arange(lon_dev, dtype=jnp.int32)
    tap_ids = jnp.arange(width + 1, dtype=jnp.int32)
    distance = jnp.abs(positions[:, None] - width - columns[None, :])
    selector = (distance[:, :, None] == tap_ids[None, None, :]).astype(jnp.float32)
    return jnp.einsum("pct,jt->jpc", selector, weights, precision=lax.Precision.HIGHEST)


def zonal_apply(padded, table):
    return jnp.einsum("ljp,jpc->ljc", padded, table, precision=lax.Precision.HIGHEST)


def lon_rim(field_in, width):
    return extended_2(field_in, (("lon", 2),), width, True)


def edge_rows(field_in):
    return jnp.concatenate([field_in, field_in], axis=1)


def merid_apply(field_in, polar, mirror_local, weights):
    rim_depth = weights.shape[0] - 1
    row_count = field_in.shape[1]
    extended = extended_2(field_in, (("lat", 1),), rim_depth, False)
    mirrored = jnp.take(polar, mirror_local, axis=2)
    north_rows = jnp.flip(mirrored[:, :rim_depth], axis=1)
    south_rows = jnp.flip(mirrored[:, rim_depth:], axis=1)
    band_index = lax.axis_index("lat")
    band_count = lax.axis_size("lat")
    upper_rim = jnp.where(band_index == 0, north_rows, extended[:, :rim_depth])
    lower_rim = jnp.where(
        band_index == band_count - 1, south_rows, extended[:, rim_depth + row_count :]
    )
    full_rows = jnp.concatenate([upper_rim, field_in, lower_rim], axis=1)
    result = weights[0] * field_in
    for offset in range(1, rim_depth + 1):
        upper = full_rows[:, rim_depth - offset : rim_depth - offset + row_count]
        lower = full_rows[:, rim_depth + offset : rim_depth + offset + row_count]
        result = result + weights[offset] * (upper + lower)
    return result


def per_device(gradient, obs_weight, half_width, zonal_coef, mirror_map, merid_coef, vertical_map):
    width = zonal_coef.shape[1] - 1
    lon_dev = gradient.shape[2]
    zonal_w = zonal_weights(half_width, zonal_coef)
    merid_w = merid_weights(merid_coef)
    table = zonal_tables(zonal_w, lon_dev)
    mirror_local = mirror_map % lon_dev
    partner_bit = lax.axis_size("lon").bit_length() - 2

    def hessian(vector):
        padded = lon_rim(vector, width)
        zonal_out = zonal_apply(padded, table)
        polar = from_partner(edge_rows(zonal_out), "lon", partner_bit)
        forward = merid_apply(zonal_out, polar, mirror_local, merid_w)
        lifted = jnp.einsum("kl,lji->kji", vertical_map, forward, precision=lax.Precision.HIGHEST)
        lowered = jnp.einsum(
            "lk,lji->kji", vertical_map, obs_weight * lifted, precision=lax.Precision.HIGHEST
        )
        returned = from_partner(edge_rows(lowered), "lon", partner_bit)
        merid_back = merid_apply(lowered, returned, mirror_local, merid_w)
        back = zonal_apply(lon_rim(merid_back, width), table)
        return vector + back

    increment = jnp.zeros_like(gradient)
    residual = gradient
    for outer in range(OUTER):
        first = hessian(residual)
        sum_rr, sum_rf, sum_ff = lax.psum(
            (jnp.sum(residual * residual), jnp.sum(residual * first), jnp.sum(first * first)),
            ("lon", "lat"),
        )
        second = hessian(first)
        sum_fs = lax.psum(jnp.sum(first * second), ("lon", "lat"))
        determinant = sum_rf * sum_fs - sum_ff * sum_ff
        coef_one = (sum_fs * sum_rr - sum_ff * sum_rf) / determinant
        coef_two = (sum_rf * sum_rf - sum_ff * sum_rr) / determinant
        increment = increment + coef_one * residual + coef_two * first
        residual = residual - coef_one * first - coef_two * second
    return (increment, residual)


def solution(mesh):
    placed = (
        P(None, "lat", "lon"),
        P(None, "lat", "lon"),
        P("lat"),
        P("lat", None),
        P("lon"),
        P(),
        P(),
    )
    return jax.shard_map(
        per_device,
        mesh=mesh,
        in_specs=placed,
        out_specs=(P(None, "lat", "lon"), P(None, "lat", "lon")),
        check_vma=False,
    )
```

profile of v0, /device:TPU:1, one launch (start us, length us, event | category | flops | bytes accessed | tf_op | source)
XLA Modules:
  0.0 373.0 jit_solution(15704041245719016282)
XLA Ops:
  1.8 2.7 collective-permute-start
  7.8 2.4 collective-permute-done
  10.3 2.7 collective-permute-done.1
  15.2 4.1 %collective-permute-start.3 = (f32[137,4,128]{2,0,1:T(8,128)S(1)}, f32[137,4,128]{2,0,1:T(8,128)}, u32[]{:S(2)}, u32[]{:S(2)}) collective-permute-start(f32[137,4,128]{2,0,1:T(8,128)S(1)} %convolution_bitcast_fusion.15), channel_id=1, source_target_pairs={{0,1},{1,2},{2,3},{4,5},{5,6},{6,7},{8,9},{9,10},{10,11},{12,13},{... | collective-permute-start | bytes 841736 | tf_op jit(solution)/shard_map/ppermute | solution.py:16
  20.5 8.2 %collective-permute-done.2 = f32[137,8,128]{2,1,0:T(8,128)S(1)} collective-permute-done((f32[137,8,128]{2,1,0:T(8,128)S(1)}, f32[137,8,128]{2,1,0:T(8,128)S(1)}, u32[]{:S(2)}, u32[]{:S(2)}) %collective-permute-start.2) | collective-permute-done | bytes 561184 | tf_op jit(solution)/shard_map/ppermute | solution.py:25
  31.7 3.9 %fusion.5 = f32[137,4,128]{2,0,1:T(8,128)S(1)} fusion(f32[137,4,128]{2,0,1:T(8,128)S(1)} %reverse_select_fusion.14, f32[137,4,128]{2,0,1:T(8,128)S(1)} %reverse_select_fusion.15, f32[137,4,128]{2,0,1:T(8,128)S(1)} %convolution_bitcast_fusion.15, f32[137,4,128]{2,1,0:T(4,128)S(1)} %copy-done.4, f32[137,137]{1,0:T(8,128)S(1)} %copy-done, f32[]{:T(128)} %bitcast.9, ...), kind=kOutput, calls=%fused_computation.29 | convolution fusion | flops 116719616 | bytes 1477976 | tf_op jit(solution)/shard_map/kl,lji->kji/dot_general | solution.py:100
  36.5 4.9 %collective-permute-start.6 = (f32[137,4,128]{2,0,1:T(8,128)S(1)}, f32[137,4,128]{2,0,1:T(8,128)}, u32[]{:S(2)}, u32[]{:S(2)}) collective-permute-start(f32[137,4,128]{2,0,1:T(8,128)S(1)} %convolution_bitcast_fusion.13), channel_id=1, source_target_pairs={{0,1},{1,2},{2,3},{4,5},{5,6},{6,7},{8,9},{9,10},{10,11},{12,13},{... | collective-permute-start | bytes 841736 | tf_op jit(solution)/shard_map/ppermute | solution.py:16
  42.7 8.1 %collective-permute-done.5 = f32[137,8,128]{2,1,0:T(8,128)S(1)} collective-permute-done((f32[137,8,128]{2,1,0:T(8,128)S(1)}, f32[137,8,128]{2,1,0:T(8,128)S(1)}, u32[]{:S(2)}, u32[]{:S(2)}) %collective-permute-start.5) | collective-permute-done | bytes 561184 | tf_op jit(solution)/shard_map/ppermute | solution.py:25
  52.7 3.5 fusion.139
  57.8 4.4 %collective-permute-done.8 = f32[137,4,32]{2,0,1:T(8,128)S(1)} collective-permute-done((f32[137,4,32]{2,0,1:T(8,128)S(1)}, f32[137,4,32]{2,0,1:T(8,128)S(1)}, u32[]{:S(2)}, u32[]{:S(2)}) %collective-permute-start.8) | collective-permute-done | bytes 70176 | tf_op jit(solution)/shard_map/ppermute | solution.py:16
  62.2 4.2 %collective-permute-done.9 = f32[137,4,32]{2,0,1:T(8,128)S(1)} collective-permute-done((f32[137,4,32]{2,0,1:T(8,128)S(1)}, f32[137,4,32]{2,0,1:T(8,128)S(1)}, u32[]{:S(2)}, u32[]{:S(2)}) %collective-permute-start.9) | collective-permute-done | bytes 70176 | tf_op jit(solution)/shard_map/ppermute | solution.py:19
  68.0 3.2 collective-permute-done.10
  71.2 5.7 %collective-permute-done.11 = f32[137,4,32]{2,0,1:T(8,128)S(1)} collective-permute-done((f32[137,4,32]{2,0,1:T(8,128)S(1)}, f32[137,4,32]{2,0,1:T(8,128)S(1)}, u32[]{:S(2)}, u32[]{:S(2)}) %collective-permute-start.11) | collective-permute-done | bytes 70176 | tf_op jit(solution)/shard_map/ppermute | solution.py:19
  78.6 5.4 %collective-permute-start.13 = (f32[137,4,128]{2,0,1:T(8,128)S(1)}, f32[137,4,128]{2,0,1:T(8,128)}, u32[]{:S(2)}, u32[]{:S(2)}) collective-permute-start(f32[137,4,128]{2,0,1:T(8,128)S(1)} %convolution_bitcast_fusion.11), channel_id=1, source_target_pairs={{0,1},{1,2},{2,3},{4,5},{5,6},{6,7},{8,9},{9,10},{10,11},{12,13},{... | collective-permute-start | bytes 841736 | tf_op jit(solution)/shard_map/ppermute | solution.py:16
  85.5 5.8 %collective-permute-done.12 = f32[137,8,128]{2,1,0:T(8,128)S(1)} collective-permute-done((f32[137,8,128]{2,1,0:T(8,128)S(1)}, f32[137,8,128]{2,1,0:T(8,128)S(1)}, u32[]{:S(2)}, u32[]{:S(2)}) %collective-permute-start.12) | collective-permute-done | bytes 561184 | tf_op jit(solution)/shard_map/ppermute | solution.py:25
  94.4 3.9 %fusion.4 = f32[137,4,128]{2,0,1:T(8,128)S(1)} fusion(f32[137,4,128]{2,0,1:T(8,128)S(1)} %reverse_select_fusion.10, f32[137,4,128]{2,0,1:T(8,128)S(1)} %reverse_select_fusion.11, f32[137,4,128]{2,0,1:T(8,128)S(1)} %convolution_bitcast_fusion.11, f32[137,4,128]{2,1,0:T(4,128)S(1)} %copy-done.5, f32[137,137]{1,0:T(8,128)S(1)} %copy-done, f32[]{:T(128)} %bitcast.9, ...), kind=kOutput, calls=%fused_computation.24 | convolution fusion | flops 116719616 | bytes 1477976 | tf_op jit(solution)/shard_map/kl,lji->kji/dot_general | solution.py:100
  100.1 6.5 %collective-permute-start.16 = (f32[137,4,128]{2,0,1:T(8,128)S(1)}, f32[137,4,128]{2,0,1:T(8,128)}, u32[]{:S(2)}, u32[]{:S(2)}) collective-permute-start(f32[137,4,128]{2,0,1:T(8,128)S(1)} %convolution_bitcast_fusion.9), channel_id=1, source_target_pairs={{0,1},{1,2},{2,3},{4,5},{5,6},{6,7},{8,9},{9,10},{10,11},{12,13},{... | collective-permute-start | bytes 841736 | tf_op jit(solution)/shard_map/ppermute | solution.py:16
  107.9 3.5 collective-permute-done.15
  113.3 2.0 collective-permute-done.17
  116.2 3.4 fusion.111
  119.8 3.8 %collective-permute-start.18 = (f32[137,4,32]{2,0,1:T(8,128)S(1)}, f32[137,4,32]{2,0,1:T(8,128)S(1)}, u32[]{:S(2)}, u32[]{:S(2)}) collective-permute-start(f32[137,4,32]{2,0,1:T(8,128)S(1)} %get-tuple-element.56), channel_id=1, source_target_pairs={{0,4},{4,8},{8,12},{12,16},{16,20},{20,24},{24,28},{28,0},{1,5},{5... | collective-permute-start | bytes 210440 | tf_op jit(solution)/shard_map/ppermute | solution.py:16
  124.4 4.1 %collective-permute-done.18 = f32[137,4,32]{2,0,1:T(8,128)S(1)} collective-permute-done((f32[137,4,32]{2,0,1:T(8,128)S(1)}, f32[137,4,32]{2,0,1:T(8,128)S(1)}, u32[]{:S(2)}, u32[]{:S(2)}) %collective-permute-start.18) | collective-permute-done | bytes 70176 | tf_op jit(solution)/shard_map/ppermute | solution.py:16
  128.4 2.8 collective-permute-done.19
  132.8 40.8 %all-reduce.1 = (f32[]{:T(128)}, f32[]{:T(128)}, f32[]{:T(128)}, f32[]{:T(128)}) all-reduce(f32[]{:T(128)} %get-tuple-element.18, f32[]{:T(128)} %get-tuple-element.19, f32[]{:T(128)} %multiply_reduce_fusion.7, f32[]{:T(128)} %get-tuple-element.17), channel_id=1, replica_groups=mesh['lon'=8,'lat'=4] {'lon','lat'}, use_global_device_ids=true, to_apply=%region_9.11 | all-reduce | flops 4 | bytes 32 | tf_op jit(solution)/shard_map/psum | solution.py:113
  181.4 3.2 collective-permute-start.20
  184.6 5.9 %collective-permute-done.20 = f32[137,4,32]{2,0,1:T(8,128)S(1)} collective-permute-done((f32[137,4,32]{2,0,1:T(8,128)S(1)}, f32[137,4,32]{2,0,1:T(8,128)S(1)}, u32[]{:S(2)}, u32[]{:S(2)}) %collective-permute-start.20) | collective-permute-done | bytes 70176 | tf_op jit(solution)/shard_map/ppermute | solution.py:16
  190.5 2.8 collective-permute-done.21
  196.1 2.3 collective-permute-start.23
  199.7 11.1 %collective-permute-done.22 = f32[137,8,128]{2,1,0:T(8,128)S(1)} collective-permute-done((f32[137,8,128]{2,1,0:T(8,128)S(1)}, f32[137,8,128]{2,1,0:T(8,128)S(1)}, u32[]{:S(2)}, u32[]{:S(2)}) %collective-permute-start.22) | collective-permute-done | bytes 561184 | tf_op jit(solution)/shard_map/ppermute | solution.py:25
  213.8 5.3 %fusion.3 = f32[137,4,128]{2,0,1:T(8,128)S(1)} fusion(f32[137,4,128]{2,0,1:T(8,128)S(1)} %reverse_select_fusion.6, f32[137,4,128]{2,0,1:T(8,128)S(1)} %reverse_select_fusion.7, f32[137,4,128]{2,0,1:T(8,128)} %convolution_bitcast_fusion.7, f32[137,4,128]{2,1,0:T(4,128)S(1)} %copy-done.6, f32[137,137]{1,0:T(8,128)S(1)} %copy-done, f32[]{:T(128)} %bitcast.9, ...), kind=kOutput, calls=%fused_computation.19 | convolution fusion | flops 116719616 | bytes 1477976 | tf_op jit(solution)/shard_map/kl,lji->kji/dot_general | solution.py:100
  220.0 3.3 collective-permute-start.26
  224.8 9.2 %collective-permute-done.25 = f32[137,8,128]{2,1,0:T(8,128)S(1)} collective-permute-done((f32[137,8,128]{2,1,0:T(8,128)S(1)}, f32[137,8,128]{2,1,0:T(8,128)S(1)}, u32[]{:S(2)}, u32[]{:S(2)}) %collective-permute-start.25) | collective-permute-done | bytes 561184 | tf_op jit(solution)/shard_map/ppermute | solution.py:25
  239.0 3.4 fusion.83
  243.9 4.0 %collective-permute-done.28 = f32[137,4,32]{2,0,1:T(8,128)S(1)} collective-permute-done((f32[137,4,32]{2,0,1:T(8,128)S(1)}, f32[137,4,32]{2,0,1:T(8,128)S(1)}, u32[]{:S(2)}, u32[]{:S(2)}) %collective-permute-start.28) | collective-permute-done | bytes 70176 | tf_op jit(solution)/shard_map/ppermute | solution.py:16
  247.9 4.5 %collective-permute-done.29 = f32[137,4,32]{2,0,1:T(8,128)S(1)} collective-permute-done((f32[137,4,32]{2,0,1:T(8,128)S(1)}, f32[137,4,32]{2,0,1:T(8,128)S(1)}, u32[]{:S(2)}, u32[]{:S(2)}) %collective-permute-start.29) | collective-permute-done | bytes 70176 | tf_op jit(solution)/shard_map/ppermute | solution.py:19
  254.7 2.4 collective-permute-done.30
  257.1 5.5 %collective-permute-done.31 = f32[137,4,32]{2,0,1:T(8,128)S(1)} collective-permute-done((f32[137,4,32]{2,0,1:T(8,128)S(1)}, f32[137,4,32]{2,0,1:T(8,128)S(1)}, u32[]{:S(2)}, u32[]{:S(2)}) %collective-permute-start.31) | collective-permute-done | bytes 70176 | tf_op jit(solution)/shard_map/ppermute | solution.py:19
  264.7 4.4 %collective-permute-start.33 = (f32[137,4,128]{2,0,1:T(8,128)S(1)}, f32[137,4,128]{2,0,1:T(8,128)}, u32[]{:S(2)}, u32[]{:S(2)}) collective-permute-start(f32[137,4,128]{2,0,1:T(8,128)S(1)} %convolution_bitcast_fusion.3), channel_id=1, source_target_pairs={{0,1},{1,2},{2,3},{4,5},{5,6},{6,7},{8,9},{9,10},{10,11},{12,13},{... | collective-permute-start | bytes 841736 | tf_op jit(solution)/shard_map/ppermute | solution.py:16
  270.4 5.9 %collective-permute-done.32 = f32[137,8,128]{2,1,0:T(8,128)} collective-permute-done((f32[137,8,128]{2,1,0:T(8,128)S(1)}, f32[137,8,128]{2,1,0:T(8,128)}, u32[]{:S(2)}, u32[]{:S(2)}) %collective-permute-start.32) | collective-permute-done | bytes 561184 | tf_op jit(solution)/shard_map/ppermute | solution.py:25
  282.3 3.8 %fusion.2 = f32[137,4,128]{2,0,1:T(8,128)S(1)} fusion(f32[137,4,128]{2,0,1:T(8,128)S(1)} %reverse_select_fusion.2, f32[137,4,128]{2,0,1:T(8,128)S(1)} %reverse_select_fusion.3, f32[137,4,128]{2,0,1:T(8,128)S(1)} %convolution_bitcast_fusion.3, f32[137,4,128]{2,1,0:T(4,128)S(1)} %copy-done.7, f32[137,137]{1,0:T(8,128)S(1)} %copy-done, f32[]{:T(128)} %bitcast.9, ...), kind=kOutput, calls=%fused_computation.14 | convolution fusion | flops 116719616 | bytes 1477976 | tf_op jit(solution)/shard_map/kl,lji->kji/dot_general | solution.py:100
  287.0 2.4 collective-permute-start.35
  289.3 4.9 %collective-permute-start.36 = (f32[137,4,128]{2,0,1:T(8,128)S(1)}, f32[137,4,128]{2,0,1:T(8,128)}, u32[]{:S(2)}, u32[]{:S(2)}) collective-permute-start(f32[137,4,128]{2,0,1:T(8,128)S(1)} %convolution_bitcast_fusion.1), channel_id=1, source_target_pairs={{0,1},{1,2},{2,3},{4,5},{5,6},{6,7},{8,9},{9,10},{10,11},{12,13},{... | collective-permute-start | bytes 841736 | tf_op jit(solution)/shard_map/ppermute | solution.py:16
  295.5 4.9 %collective-permute-done.35 = f32[137,8,128]{2,1,0:T(8,128)} collective-permute-done((f32[137,8,128]{2,1,0:T(8,128)S(1)}, f32[137,8,128]{2,1,0:T(8,128)}, u32[]{:S(2)}, u32[]{:S(2)}) %collective-permute-start.35) | collective-permute-done | bytes 561184 | tf_op jit(solution)/shard_map/ppermute | solution.py:25
  305.5 3.4 fusion.55
  309.1 4.0 %collective-permute-start.38 = (f32[137,4,32]{2,0,1:T(8,128)S(1)}, f32[137,4,32]{2,0,1:T(8,128)S(1)}, u32[]{:S(2)}, u32[]{:S(2)}) collective-permute-start(f32[137,4,32]{2,0,1:T(8,128)S(1)} %get-tuple-element.48), channel_id=1, source_target_pairs={{0,4},{4,8},{8,12},{12,16},{16,20},{20,24},{24,28},{28,0},{1,5},{5... | collective-permute-start | bytes 210440 | tf_op jit(solution)/shard_map/ppermute | solution.py:16
  313.1 5.2 %collective-permute-done.38 = f32[137,4,32]{2,0,1:T(8,128)S(1)} collective-permute-done((f32[137,4,32]{2,0,1:T(8,128)S(1)}, f32[137,4,32]{2,0,1:T(8,128)S(1)}, u32[]{:S(2)}, u32[]{:S(2)}) %collective-permute-start.38) | collective-permute-done | bytes 70176 | tf_op jit(solution)/shard_map/ppermute | solution.py:16
  318.3 3.3 collective-permute-done.39
  323.1 40.2 %all-reduce = (f32[]{:T(128)}, f32[]{:T(128)}, f32[]{:T(128)}, f32[]{:T(128)}) all-reduce(f32[]{:T(128)} %get-tuple-element.14, f32[]{:T(128)} %get-tuple-element.16, f32[]{:T(128)} %get-tuple-element.15, f32[]{:T(128)} %get-tuple-element.13), channel_id=1, replica_groups=mesh['lon'=8,'lat'=4] {'lon','lat'}, use_global_device_ids=true, to_apply=%region_17.19 | all-reduce | flops 4 | bytes 32 | tf_op jit(solution)/shard_map/psum | solution.py:113
  (173 shorter events, 70.0 us)
Async XLA Ops:
  0.6 31.0 %copy-start = (f32[137,137]{1,0:T(8,128)S(1)}, f32[137,137]{1,0:T(8,128)}, u32[]{:S(2)}) copy-start(f32[137,137]{1,0:T(8,128)} %param.15) | copy-start | bytes 225232
  0.6 3.9 %copy-start.3 = (s32[4]{0:T(128)S(1)}, s32[4]{0:T(128)}, u32[]{:S(2)}) copy-start(s32[4]{0:T(128)} %param.11) | copy-start | bytes 52
  0.7 3.8 %copy-start.2 = (f32[4,33]{1,0:T(4,128)S(1)}, f32[4,33]{1,0:T(4,128)}, u32[]{:S(2)}) copy-start(f32[4,33]{1,0:T(4,128)} %param.12) | copy-start | bytes 1588
  0.7 4.4 %copy-start.9 = (f32[5]{0:T(128)S(1)}, f32[5]{0:T(128)}, u32[]{:S(2)}) copy-start(f32[5]{0:T(128)} %param.14) | copy-start | bytes 64
  1.8 8.4 %collective-permute-start = (f32[137,4,32]{2,0,1:T(8,128)S(1)}, f32[137,4,32]{2,0,1:T(8,128)S(1)}, u32[]{:S(2)}, u32[]{:S(2)}) collective-permute-start(f32[137,4,32]{2,0,1:T(8,128)S(1)} %get-tuple-element.62), channel_id=1, source_target_pairs={{0,4},{4,8},{8,12},{12,16},{16,20},{20,24},{24,28},{28,0},{1,5},{5... | collective-permute-start | bytes 210440 | tf_op jit(solution)/shard_map/ppermute | solution.py:16
  4.5 8.5 %collective-permute-start.1 = (f32[137,4,32]{2,0,1:T(8,128)S(1)}, f32[137,4,32]{2,0,1:T(8,128)S(1)}, u32[]{:S(2)}, u32[]{:S(2)}) collective-permute-start(f32[137,4,32]{2,0,1:T(8,128)S(1)} %get-tuple-element.63), channel_id=1, source_target_pairs={{4,0},{8,4},{12,8},{16,12},{20,16},{24,20},{28,24},{0,28},{5,1},{9... | collective-permute-start | bytes 210440 | tf_op jit(solution)/shard_map/ppermute | solution.py:19
  14.0 14.7 %collective-permute-start.2 = (f32[137,8,128]{2,1,0:T(8,128)S(1)}, f32[137,8,128]{2,1,0:T(8,128)S(1)}, u32[]{:S(2)}, u32[]{:S(2)}) collective-permute-start(f32[137,8,128]{2,1,0:T(8,128)S(1)} %copy.185), channel_id=1, source_target_pairs={{0,16},{4,20},{8,24},{12,28},{16,0},{20,4},{24,8},{28,12},{1,17},{... | collective-permute-start | bytes 1683464 | tf_op jit(solution)/shard_map/ppermute | solution.py:25
  15.2 15.4 %collective-permute-start.3 = (f32[137,4,128]{2,0,1:T(8,128)S(1)}, f32[137,4,128]{2,0,1:T(8,128)}, u32[]{:S(2)}, u32[]{:S(2)}) collective-permute-start(f32[137,4,128]{2,0,1:T(8,128)S(1)} %convolution_bitcast_fusion.15), channel_id=1, source_target_pairs={{0,1},{1,2},{2,3},{4,5},{5,6},{6,7},{8,9},{9,10},{10,11},{12,13},{... | collective-permute-start | bytes 841736 | tf_op jit(solution)/shard_map/ppermute | solution.py:16
  19.2 11.4 %collective-permute-start.4 = (f32[137,4,128]{2,0,1:T(8,128)S(1)}, f32[137,4,128]{2,0,1:T(8,128)}, u32[]{:S(2)}, u32[]{:S(2)}) collective-permute-start(f32[137,4,128]{2,0,1:T(8,128)S(1)} %convolution_bitcast_fusion.15), channel_id=1, source_target_pairs={{1,0},{2,1},{3,2},{5,4},{6,5},{7,6},{9,8},{10,9},{11,10},{13,12},{... | collective-permute-start | bytes 841736 | tf_op jit(solution)/shard_map/ppermute | solution.py:19
  30.6 1.1 copy-start.4
  36.4 14.4 %collective-permute-start.5 = (f32[137,8,128]{2,1,0:T(8,128)S(1)}, f32[137,8,128]{2,1,0:T(8,128)S(1)}, u32[]{:S(2)}, u32[]{:S(2)}) collective-permute-start(f32[137,8,128]{2,1,0:T(8,128)S(1)} %copy.190), channel_id=1, source_target_pairs={{0,16},{4,20},{8,24},{12,28},{16,0},{20,4},{24,8},{28,12},{1,17},{... | collective-permute-start | bytes 1683464 | tf_op jit(solution)/shard_map/ppermute | solution.py:25
  36.5 16.1 %collective-permute-start.6 = (f32[137,4,128]{2,0,1:T(8,128)S(1)}, f32[137,4,128]{2,0,1:T(8,128)}, u32[]{:S(2)}, u32[]{:S(2)}) collective-permute-start(f32[137,4,128]{2,0,1:T(8,128)S(1)} %convolution_bitcast_fusion.13), channel_id=1, source_target_pairs={{0,1},{1,2},{2,3},{4,5},{5,6},{6,7},{8,9},{9,10},{10,11},{12,13},{... | collective-permute-start | bytes 841736 | tf_op jit(solution)/shard_map/ppermute | solution.py:16
  41.4 11.3 %collective-permute-start.7 = (f32[137,4,128]{2,0,1:T(8,128)S(1)}, f32[137,4,128]{2,0,1:T(8,128)S(1)}, u32[]{:S(2)}, u32[]{:S(2)}) collective-permute-start(f32[137,4,128]{2,0,1:T(8,128)S(1)} %convolution_bitcast_fusion.13), channel_id=1, source_target_pairs={{1,0},{2,1},{3,2},{5,4},{6,5},{7,6},{9,8},{10,9},{11,10},{13,12},{... | collective-permute-start | bytes 841736 | tf_op jit(solution)/shard_map/ppermute | solution.py:19
  52.7 13.7 %copy-start.1 = (f32[137,4,128]{2,1,0:T(4,128)S(1)}, f32[137,4,128]{2,1,0:T(4,128)}, u32[]{:S(2)}) copy-start(f32[137,4,128]{2,1,0:T(4,128)} %param.9) | copy-start | bytes 841732
  56.3 5.9 %collective-permute-start.8 = (f32[137,4,32]{2,0,1:T(8,128)S(1)}, f32[137,4,32]{2,0,1:T(8,128)S(1)}, u32[]{:S(2)}, u32[]{:S(2)}) collective-permute-start(f32[137,4,32]{2,0,1:T(8,128)S(1)} %get-tuple-element.60), channel_id=1, source_target_pairs={{0,4},{4,8},{8,12},{12,16},{16,20},{20,24},{24,28},{28,0},{1,5},{5... | collective-permute-start | bytes 210440 | tf_op jit(solution)/shard_map/ppermute | solution.py:16
  57.8 8.7 %collective-permute-start.9 = (f32[137,4,32]{2,0,1:T(8,128)S(1)}, f32[137,4,32]{2,0,1:T(8,128)S(1)}, u32[]{:S(2)}, u32[]{:S(2)}) collective-permute-start(f32[137,4,32]{2,0,1:T(8,128)S(1)} %get-tuple-element.61), channel_id=1, source_target_pairs={{4,0},{8,4},{12,8},{16,12},{20,16},{24,20},{28,24},{0,28},{5,1},{9... | collective-permute-start | bytes 210440 | tf_op jit(solution)/shard_map/ppermute | solution.py:19
  67.4 3.7 collective-permute-start.10
  67.5 9.4 %collective-permute-start.11 = (f32[137,4,32]{2,0,1:T(8,128)S(1)}, f32[137,4,32]{2,0,1:T(8,128)S(1)}, u32[]{:S(2)}, u32[]{:S(2)}) collective-permute-start(f32[137,4,32]{2,0,1:T(8,128)S(1)} %get-tuple-element.59), channel_id=1, source_target_pairs={{4,0},{8,4},{12,8},{16,12},{20,16},{24,20},{28,24},{0,28},{5,1},{9... | collective-permute-start | bytes 210440 | tf_op jit(solution)/shard_map/ppermute | solution.py:19
  77.9 13.4 %collective-permute-start.12 = (f32[137,8,128]{2,1,0:T(8,128)S(1)}, f32[137,8,128]{2,1,0:T(8,128)S(1)}, u32[]{:S(2)}, u32[]{:S(2)}) collective-permute-start(f32[137,8,128]{2,1,0:T(8,128)S(1)} %copy.196), channel_id=1, source_target_pairs={{0,16},{4,20},{8,24},{12,28},{16,0},{20,4},{24,8},{28,12},{1,17},{... | collective-permute-start | bytes 1683464 | tf_op jit(solution)/shard_map/ppermute | solution.py:25
  78.6 14.5 %collective-permute-start.13 = (f32[137,4,128]{2,0,1:T(8,128)S(1)}, f32[137,4,128]{2,0,1:T(8,128)}, u32[]{:S(2)}, u32[]{:S(2)}) collective-permute-start(f32[137,4,128]{2,0,1:T(8,128)S(1)} %convolution_bitcast_fusion.11), channel_id=1, source_target_pairs={{0,1},{1,2},{2,3},{4,5},{5,6},{6,7},{8,9},{9,10},{10,11},{12,13},{... | collective-permute-start | bytes 841736 | tf_op jit(solution)/shard_map/ppermute | solution.py:16
  84.0 9.4 %collective-permute-start.14 = (f32[137,4,128]{2,0,1:T(8,128)S(1)}, f32[137,4,128]{2,0,1:T(8,128)}, u32[]{:S(2)}, u32[]{:S(2)}) collective-permute-start(f32[137,4,128]{2,0,1:T(8,128)S(1)} %convolution_bitcast_fusion.11), channel_id=1, source_target_pairs={{1,0},{2,1},{3,2},{5,4},{6,5},{7,6},{9,8},{10,9},{11,10},{13,12},{... | collective-permute-start | bytes 841736 | tf_op jit(solution)/shard_map/ppermute | solution.py:19
  93.2 1.2 copy-start.5
  99.1 12.2 %collective-permute-start.15 = (f32[137,8,128]{2,1,0:T(8,128)S(1)}, f32[137,8,128]{2,1,0:T(8,128)S(1)}, u32[]{:S(2)}, u32[]{:S(2)}) collective-permute-start(f32[137,8,128]{2,1,0:T(8,128)S(1)} %copy.201), channel_id=1, source_target_pairs={{0,16},{4,20},{8,24},{12,28},{16,0},{20,4},{24,8},{28,12},{1,17},{... | collective-permute-start | bytes 1683464 | tf_op jit(solution)/shard_map/ppermute | solution.py:25
  100.1 13.1 %collective-permute-start.16 = (f32[137,4,128]{2,0,1:T(8,128)S(1)}, f32[137,4,128]{2,0,1:T(8,128)}, u32[]{:S(2)}, u32[]{:S(2)}) collective-permute-start(f32[137,4,128]{2,0,1:T(8,128)S(1)} %convolution_bitcast_fusion.9), channel_id=1, source_target_pairs={{0,1},{1,2},{2,3},{4,5},{5,6},{6,7},{8,9},{9,10},{10,11},{12,13},{... | collective-permute-start | bytes 841736 | tf_op jit(solution)/shard_map/ppermute | solution.py:16
  106.6 8.6 %collective-permute-start.17 = (f32[137,4,128]{2,0,1:T(8,128)S(1)}, f32[137,4,128]{2,0,1:T(8,128)}, u32[]{:S(2)}, u32[]{:S(2)}) collective-permute-start(f32[137,4,128]{2,0,1:T(8,128)S(1)} %convolution_bitcast_fusion.9), channel_id=1, source_target_pairs={{1,0},{2,1},{3,2},{5,4},{6,5},{7,6},{9,8},{10,9},{11,10},{13,12},{... | collective-permute-start | bytes 841736 | tf_op jit(solution)/shard_map/ppermute | solution.py:19
  119.8 8.6 %collective-permute-start.18 = (f32[137,4,32]{2,0,1:T(8,128)S(1)}, f32[137,4,32]{2,0,1:T(8,128)S(1)}, u32[]{:S(2)}, u32[]{:S(2)}) collective-permute-start(f32[137,4,32]{2,0,1:T(8,128)S(1)} %get-tuple-element.56), channel_id=1, source_target_pairs={{0,4},{4,8},{8,12},{12,16},{16,20},{20,24},{24,28},{28,0},{1,5},{5... | collective-permute-start | bytes 210440 | tf_op jit(solution)/shard_map/ppermute | solution.py:16
  123.6 7.7 %collective-permute-start.19 = (f32[137,4,32]{2,0,1:T(8,128)S(1)}, f32[137,4,32]{2,0,1:T(8,128)S(1)}, u32[]{:S(2)}, u32[]{:S(2)}) collective-permute-start(f32[137,4,32]{2,0,1:T(8,128)S(1)} %get-tuple-element.57), channel_id=1, source_target_pairs={{4,0},{8,4},{12,8},{16,12},{20,16},{24,20},{28,24},{0,28},{5,1},{9... | collective-permute-start | bytes 210440 | tf_op jit(solution)/shard_map/ppermute | solution.py:19
  181.4 9.1 %collective-permute-start.20 = (f32[137,4,32]{2,0,1:T(8,128)S(1)}, f32[137,4,32]{2,0,1:T(8,128)S(1)}, u32[]{:S(2)}, u32[]{:S(2)}) collective-permute-start(f32[137,4,32]{2,0,1:T(8,128)S(1)} %get-tuple-element.54), channel_id=1, source_target_pairs={{0,4},{4,8},{8,12},{12,16},{16,20},{20,24},{24,28},{28,0},{1,5},{5... | collective-permute-start | bytes 210440 | tf_op jit(solution)/shard_map/ppermute | solution.py:16
  184.6 8.7 %collective-permute-start.21 = (f32[137,4,32]{2,0,1:T(8,128)S(1)}, f32[137,4,32]{2,0,1:T(8,128)S(1)}, u32[]{:S(2)}, u32[]{:S(2)}) collective-permute-start(f32[137,4,32]{2,0,1:T(8,128)S(1)} %get-tuple-element.55), channel_id=1, source_target_pairs={{4,0},{8,4},{12,8},{16,12},{20,16},{24,20},{28,24},{0,28},{5,1},{9... | collective-permute-start | bytes 210440 | tf_op jit(solution)/shard_map/ppermute | solution.py:19
  196.0 14.8 %collective-permute-start.22 = (f32[137,8,128]{2,1,0:T(8,128)S(1)}, f32[137,8,128]{2,1,0:T(8,128)S(1)}, u32[]{:S(2)}, u32[]{:S(2)}) collective-permute-start(f32[137,8,128]{2,1,0:T(8,128)S(1)} %copy.209), channel_id=1, source_target_pairs={{0,16},{4,20},{8,24},{12,28},{16,0},{20,4},{24,8},{28,12},{1,17},{... | collective-permute-start | bytes 1683464 | tf_op jit(solution)/shard_map/ppermute | solution.py:25
  196.1 16.6 %collective-permute-start.23 = (f32[137,4,128]{2,0,1:T(8,128)}, f32[137,4,128]{2,0,1:T(8,128)}, u32[]{:S(2)}, u32[]{:S(2)}) collective-permute-start(f32[137,4,128]{2,0,1:T(8,128)} %convolution_bitcast_fusion.7), channel_id=1, source_target_pairs={{0,1},{1,2},{2,3},{4,5},{5,6},{6,7},{8,9},{9,10},{10,11},{12,13},{... | collective-permute-start | bytes 841736 | tf_op jit(solution)/shard_map/ppermute | solution.py:16
  198.4 14.3 %collective-permute-start.24 = (f32[137,4,128]{2,0,1:T(8,128)}, f32[137,4,128]{2,0,1:T(8,128)}, u32[]{:S(2)}, u32[]{:S(2)}) collective-permute-start(f32[137,4,128]{2,0,1:T(8,128)} %convolution_bitcast_fusion.7), channel_id=1, source_target_pairs={{1,0},{2,1},{3,2},{5,4},{6,5},{7,6},{9,8},{10,9},{11,10},{13,12},{... | collective-permute-start | bytes 841736 | tf_op jit(solution)/shard_map/ppermute | solution.py:19
  212.7 1.1 copy-start.6
  219.9 14.0 %collective-permute-start.25 = (f32[137,8,128]{2,1,0:T(8,128)S(1)}, f32[137,8,128]{2,1,0:T(8,128)S(1)}, u32[]{:S(2)}, u32[]{:S(2)}) collective-permute-start(f32[137,8,128]{2,1,0:T(8,128)S(1)} %copy.214), channel_id=1, source_target_pairs={{0,16},{4,20},{8,24},{12,28},{16,0},{20,4},{24,8},{28,12},{1,17},{... | collective-permute-start | bytes 1683464 | tf_op jit(solution)/shard_map/ppermute | solution.py:25
  220.0 17.9 %collective-permute-start.26 = (f32[137,4,128]{2,0,1:T(8,128)S(1)}, f32[137,4,128]{2,0,1:T(8,128)}, u32[]{:S(2)}, u32[]{:S(2)}) collective-permute-start(f32[137,4,128]{2,0,1:T(8,128)S(1)} %convolution_bitcast_fusion.5), channel_id=1, source_target_pairs={{0,1},{1,2},{2,3},{4,5},{5,6},{6,7},{8,9},{9,10},{10,11},{12,13},{... | collective-permute-start | bytes 841736 | tf_op jit(solution)/shard_map/ppermute | solution.py:16
  223.3 14.7 %collective-permute-start.27 = (f32[137,4,128]{2,0,1:T(8,128)S(1)}, f32[137,4,128]{2,0,1:T(8,128)}, u32[]{:S(2)}, u32[]{:S(2)}) collective-permute-start(f32[137,4,128]{2,0,1:T(8,128)S(1)} %convolution_bitcast_fusion.5), channel_id=1, source_target_pairs={{1,0},{2,1},{3,2},{5,4},{6,5},{7,6},{9,8},{10,9},{11,10},{13,12},{... | collective-permute-start | bytes 841736 | tf_op jit(solution)/shard_map/ppermute | solution.py:19
  242.6 5.3 %collective-permute-start.28 = (f32[137,4,32]{2,0,1:T(8,128)S(1)}, f32[137,4,32]{2,0,1:T(8,128)S(1)}, u32[]{:S(2)}, u32[]{:S(2)}) collective-permute-start(f32[137,4,32]{2,0,1:T(8,128)S(1)} %get-tuple-element.52), channel_id=1, source_target_pairs={{0,4},{4,8},{8,12},{12,16},{16,20},{20,24},{24,28},{28,0},{1,5},{5... | collective-permute-start | bytes 210440 | tf_op jit(solution)/shard_map/ppermute | solution.py:16
  243.8 8.5 %collective-permute-start.29 = (f32[137,4,32]{2,0,1:T(8,128)S(1)}, f32[137,4,32]{2,0,1:T(8,128)S(1)}, u32[]{:S(2)}, u32[]{:S(2)}) collective-permute-start(f32[137,4,32]{2,0,1:T(8,128)S(1)} %get-tuple-element.53), channel_id=1, source_target_pairs={{4,0},{8,4},{12,8},{16,12},{20,16},{24,20},{28,24},{0,28},{5,1},{9... | collective-permute-start | bytes 210440 | tf_op jit(solution)/shard_map/ppermute | solution.py:19
  253.4 3.7 collective-permute-start.30
  253.4 9.1 %collective-permute-start.31 = (f32[137,4,32]{2,0,1:T(8,128)S(1)}, f32[137,4,32]{2,0,1:T(8,128)S(1)}, u32[]{:S(2)}, u32[]{:S(2)}) collective-permute-start(f32[137,4,32]{2,0,1:T(8,128)S(1)} %get-tuple-element.51), channel_id=1, source_target_pairs={{4,0},{8,4},{12,8},{16,12},{20,16},{24,20},{28,24},{0,28},{5,1},{9... | collective-permute-start | bytes 210440 | tf_op jit(solution)/shard_map/ppermute | solution.py:19
  263.6 12.7 %collective-permute-start.32 = (f32[137,8,128]{2,1,0:T(8,128)S(1)}, f32[137,8,128]{2,1,0:T(8,128)}, u32[]{:S(2)}, u32[]{:S(2)}) collective-permute-start(f32[137,8,128]{2,1,0:T(8,128)S(1)} %copy.219), channel_id=1, source_target_pairs={{0,16},{4,20},{8,24},{12,28},{16,0},{20,4},{24,8},{28,12},{1,17},{... | collective-permute-start | bytes 1683464 | tf_op jit(solution)/shard_map/ppermute | solution.py:25
  264.7 16.6 %collective-permute-start.33 = (f32[137,4,128]{2,0,1:T(8,128)S(1)}, f32[137,4,128]{2,0,1:T(8,128)}, u32[]{:S(2)}, u32[]{:S(2)}) collective-permute-start(f32[137,4,128]{2,0,1:T(8,128)S(1)} %convolution_bitcast_fusion.3), channel_id=1, source_target_pairs={{0,1},{1,2},{2,3},{4,5},{5,6},{6,7},{8,9},{9,10},{10,11},{12,13},{... | collective-permute-start | bytes 841736 | tf_op jit(solution)/shard_map/ppermute | solution.py:16
  269.1 12.2 %collective-permute-start.34 = (f32[137,4,128]{2,0,1:T(8,128)S(1)}, f32[137,4,128]{2,0,1:T(8,128)S(1)}, u32[]{:S(2)}, u32[]{:S(2)}) collective-permute-start(f32[137,4,128]{2,0,1:T(8,128)S(1)} %convolution_bitcast_fusion.3), channel_id=1, source_target_pairs={{1,0},{2,1},{3,2},{5,4},{6,5},{7,6},{9,8},{10,9},{11,10},{13,12},{... | collective-permute-start | bytes 841736 | tf_op jit(solution)/shard_map/ppermute | solution.py:19
  287.0 13.5 %collective-permute-start.35 = (f32[137,8,128]{2,1,0:T(8,128)S(1)}, f32[137,8,128]{2,1,0:T(8,128)}, u32[]{:S(2)}, u32[]{:S(2)}) collective-permute-start(f32[137,8,128]{2,1,0:T(8,128)S(1)} %copy.224), channel_id=1, source_target_pairs={{0,16},{4,20},{8,24},{12,28},{16,0},{20,4},{24,8},{28,12},{1,17},{... | collective-permute-start | bytes 1683464 | tf_op jit(solution)/shard_map/ppermute | solution.py:25
  289.3 16.1 %collective-permute-start.36 = (f32[137,4,128]{2,0,1:T(8,128)S(1)}, f32[137,4,128]{2,0,1:T(8,128)}, u32[]{:S(2)}, u32[]{:S(2)}) collective-permute-start(f32[137,4,128]{2,0,1:T(8,128)S(1)} %convolution_bitcast_fusion.1), channel_id=1, source_target_pairs={{0,1},{1,2},{2,3},{4,5},{5,6},{6,7},{8,9},{9,10},{10,11},{12,13},{... | collective-permute-start | bytes 841736 | tf_op jit(solution)/shard_map/ppermute | solution.py:16
  294.2 11.3 %collective-permute-start.37 = (f32[137,4,128]{2,0,1:T(8,128)S(1)}, f32[137,4,128]{2,0,1:T(8,128)S(1)}, u32[]{:S(2)}, u32[]{:S(2)}) collective-permute-start(f32[137,4,128]{2,0,1:T(8,128)S(1)} %convolution_bitcast_fusion.1), channel_id=1, source_target_pairs={{1,0},{2,1},{3,2},{5,4},{6,5},{7,6},{9,8},{10,9},{11,10},{13,12},{... | collective-permute-start | bytes 841736 | tf_op jit(solution)/shard_map/ppermute | solution.py:19
  309.1 9.2 %collective-permute-start.38 = (f32[137,4,32]{2,0,1:T(8,128)S(1)}, f32[137,4,32]{2,0,1:T(8,128)S(1)}, u32[]{:S(2)}, u32[]{:S(2)}) collective-permute-start(f32[137,4,32]{2,0,1:T(8,128)S(1)} %get-tuple-element.48), channel_id=1, source_target_pairs={{0,4},{4,8},{8,12},{12,16},{16,20},{20,24},{24,28},{28,0},{1,5},{5... | collective-permute-start | bytes 210440 | tf_op jit(solution)/shard_map/ppermute | solution.py:16
  313.1 8.5 %collective-permute-start.39 = (f32[137,4,32]{2,0,1:T(8,128)S(1)}, f32[137,4,32]{2,0,1:T(8,128)S(1)}, u32[]{:S(2)}, u32[]{:S(2)}) collective-permute-start(f32[137,4,32]{2,0,1:T(8,128)S(1)} %get-tuple-element.49), channel_id=1, source_target_pairs={{4,0},{8,4},{12,8},{16,12},{20,16},{24,20},{28,24},{0,28},{5,1},{9... | collective-permute-start | bytes 210440 | tf_op jit(solution)/shard_map/ppermute | solution.py:19
  (2 other events, 1.6 us)
where the time goes:
time: 376 us; the launch traced here: 373 us
  waiting for transfers between devices  122 us (32%)
  blocking collectives  80.9 us (22%)
  starting transfers between devices  70.1 us (19%)
  local copies, waits for them, and re-layouts  29.9 us (8%)
  matrix products  29.1 us (8%)
  other arithmetic  23 us (6%)
  between operations  18 us (5%)
    psum x2, blocking collectives, per_device(): lax.psum((jnp.sum(residual * residual), jnp.sum(residual * first), jnp.su...  80.9 us
    ppermute x8, waiting for transfers between devices, from_partner(): lax.ppermute(value, axis, [(i, i ^ 1 << distance) for i in range(lax.axis...  56.7 us
    ppermute x16, starting transfers between devices, extended_2(): lax.ppermute(lax.slice_in_dim(block, block.shape[dim] - width, None, axis...  52.2 us
    ppermute x16, waiting for transfers between devices, extended_2(): lax.ppermute(lax.slice_in_dim(block, 0, width, axis=dim), axis, backward)  33.7 us
    ppermute x16, waiting for transfers between devices, extended_2(): lax.ppermute(lax.slice_in_dim(block, block.shape[dim] - width, None, axis...  31.7 us
    dot_general x4, matrix products, hessian(): jnp.einsum('kl,lji->kji', vertical_map, forward, precision=lax.Precision....  16.8 us
    gather x16, local copies, waits for them, and re-layouts, merid_apply(): mirrored = jnp.take(polar, mirror_local, axis=2)  16 us
    add x4, other arithmetic, merid_apply(): result = result + weights[offset] * (upper + lower)  13.7 us
  transfers between devices with their start and end apart: 40, of which 26 were waited for; matrix products, arithmetic and copies ran while one was open for 7% of the time, Pallas kernels for 0%

commit v1 on v0

v1 whole, which is shorter than its diff:
```python
import jax
import jax.numpy as jnp
from jax import lax
from jax.sharding import PartitionSpec as P

OUTER = 2
AXES = ("lon", "lat")
HI = lax.Precision.HIGHEST


def zonal_weights(half_width, zonal_coef):
    tap_ids = jnp.arange(zonal_coef.shape[1], dtype=jnp.int32)
    kept = jnp.where(
        tap_ids[None, :] <= half_width[:, None], zonal_coef, jnp.zeros_like(zonal_coef)
    )
    scaling = jnp.sqrt(kept[:, 0] ** 2 + 2.0 * jnp.sum(kept[:, 1:] ** 2, axis=1))
    return kept / scaling[:, None]


def merid_weights(merid_coef):
    norm_value = jnp.sqrt(merid_coef[0] ** 2 + 2.0 * jnp.sum(merid_coef[1:] ** 2))
    return merid_coef / norm_value


def zonal_tables(weights, block):
    width = weights.shape[1] - 1
    positions = jnp.arange(block + 2 * width, dtype=jnp.int32)
    columns = jnp.arange(block, dtype=jnp.int32)
    tap_ids = jnp.arange(width + 1, dtype=jnp.int32)
    distance = jnp.abs(positions[:, None] - width - columns[None, :])
    selector = (distance[:, :, None] == tap_ids[None, None, :]).astype(jnp.float32)
    return jnp.einsum("pct,jt->jpc", selector, weights, precision=HI)


def zonal_level(field_in, table, block):
    lev, rows, nlon = field_in.shape
    width = (table.shape[1] - block) // 2
    blocks = field_in.reshape(lev, rows, nlon // block, block)
    before = jnp.roll(blocks, 1, axis=2)[..., block - width :]
    after = jnp.roll(blocks, -1, axis=2)[..., :width]
    padded = jnp.concatenate([before, blocks, after], axis=3)
    out = jnp.einsum("ljbp,jpc->ljbc", padded, table, precision=HI)
    return out.reshape(lev, rows, nlon)


def merid_level(field_in, weights, mirror_map):
    rim_depth = weights.shape[0] - 1
    row_count = field_in.shape[1]
    north_rows = jnp.take(jnp.flip(field_in[:, :rim_depth], axis=1), mirror_map, axis=2)
    south_rows = jnp.take(
        jnp.flip(field_in[:, row_count - rim_depth :], axis=1), mirror_map, axis=2
    )
    extended = jnp.concatenate([north_rows, field_in, south_rows], axis=1)
    result = weights[0] * field_in
    for offset in range(1, rim_depth + 1):
        upper = extended[:, rim_depth - offset : rim_depth - offset + row_count]
        lower = extended[:, rim_depth + offset : rim_depth + offset + row_count]
        result = result + weights[offset] * (upper + lower)
    return result


def per_device(gradient, obs_weight, half_width, zonal_coef, mirror_map, merid_coef, vertical_map):
    n_lon = lax.axis_size("lon")
    n_lat = lax.axis_size("lat")
    n_dev = n_lon * n_lat
    lev, rows, cols = gradient.shape
    per = -(-lev // n_dev)
    width = zonal_coef.shape[1] - 1
    merid_w = merid_weights(merid_coef)

    def exchange(parts):
        return lax.all_to_all(parts, AXES, 0, 0, tiled=True)

    def col_parts(x):
        x = jnp.pad(x, ((0, n_dev * per - lev), (0, 0), (0, 0)))
        return x.reshape(n_dev, per, rows, cols)

    def to_level(z):
        z = z.reshape(n_lon, n_lat, per, rows, cols).transpose(2, 1, 3, 0, 4)
        return z.reshape(per, n_lat * rows, n_lon * cols)

    def level_parts(v):
        v = v.reshape(per, n_lat, rows, n_lon, cols).transpose(3, 1, 0, 2, 4)
        return v.reshape(n_dev, per, rows, cols)

    def to_column(z):
        return z.reshape(n_dev * per, rows, cols)[:lev]

    def slab(values):
        flat = jnp.zeros((rows * cols,), jnp.float32).at[: values.shape[0]].set(values)
        return jnp.broadcast_to(flat.reshape(1, 1, rows, cols), (n_dev, 1, rows, cols))

    mirror_slab = jnp.zeros((1, 1, rows, cols), jnp.float32).at[0, 0, 0].set(
        mirror_map.astype(jnp.float32)
    )
    zonal_slab = jnp.zeros((1, 1, rows, cols), jnp.float32).at[0, 0, :, : width + 1].set(
        zonal_weights(half_width, zonal_coef)
    )
    got = exchange(
        jnp.concatenate(
            [
                col_parts(gradient),
                jnp.broadcast_to(mirror_slab, (n_dev, 1, rows, cols)),
                jnp.broadcast_to(zonal_slab, (n_dev, 1, rows, cols)),
            ],
            axis=1,
        )
    )
    residual = to_level(got[:, :per])
    mirror_all = (
        got[:, per, 0, :].reshape(n_lon, n_lat, cols)[:, 0].reshape(n_lon * cols).astype(jnp.int32)
    )
    zonal_all = (
        got[:, per + 1, :, : width + 1]
        .reshape(n_lon, n_lat, rows, width + 1)[0]
        .reshape(n_lat * rows, width + 1)
    )
    table = zonal_tables(zonal_all, cols)

    def forward(x):
        return merid_level(zonal_level(x, table, cols), merid_w, mirror_all)

    def backward(g):
        return zonal_level(merid_level(g, merid_w, mirror_all), table, cols)

    def middle(y):
        lifted = jnp.einsum("kl,lji->kji", vertical_map, y, precision=HI)
        return jnp.einsum("lk,lji->kji", vertical_map, obs_weight * lifted, precision=HI)

    def image(x, px_col):
        return x + backward(to_level(exchange(col_parts(middle(px_col)))))

    res_col = gradient
    inc_col = jnp.zeros_like(gradient)
    pres_col = to_column(exchange(level_parts(forward(residual))))
    for outer in range(OUTER):
        last = outer == OUTER - 1
        first = image(residual, pres_col)
        got = exchange(jnp.concatenate([level_parts(forward(first)), level_parts(first)], axis=1))
        pfirst_col = to_column(got[:, :per])
        first_col = to_column(got[:, per:])
        second = image(first, pfirst_col)
        sums = jnp.stack(
            [
                jnp.sum(residual * residual),
                jnp.sum(residual * first),
                jnp.sum(first * first),
                jnp.sum(first * second),
            ]
        )
        parts = [level_parts(second)]
        if not last:
            parts.append(level_parts(forward(second)))
        got = exchange(jnp.concatenate(parts + [slab(sums)], axis=1))
        second_col = to_column(got[:, :per])
        total = jnp.sum(got[:, len(parts) * per, 0, : sums.shape[0]], axis=0)
        sum_rr, sum_rf, sum_ff, sum_fs = total[0], total[1], total[2], total[3]
        determinant = sum_rf * sum_fs - sum_ff * sum_ff
        coef_one = (sum_fs * sum_rr - sum_ff * sum_rf) / determinant
        coef_two = (sum_rf * sum_rf - sum_ff * sum_rr) / determinant
        inc_col = inc_col + coef_one * res_col + coef_two * first_col
        res_col = res_col - coef_one * first_col - coef_two * second_col
        if not last:
            psecond_col = to_column(got[:, per : 2 * per])
            residual = residual - coef_one * first - coef_two * second
            pres_col = pres_col - coef_one * pfirst_col - coef_two * psecond_col
    return (inc_col, res_col)


def solution(mesh):
    placed = (
        P(None, "lat", "lon"),
        P(None, "lat", "lon"),
        P("lat"),
        P("lat", None),
        P("lon"),
        P(),
        P(),
    )
    return jax.shard_map(
        per_device,
        mesh=mesh,
        in_specs=placed,
        out_specs=(P(None, "lat", "lon"), P(None, "lat", "lon")),
        check_vma=False,
    )
```

time: 376 us -> 662 us (1.76); the launches traced: 373 us -> 650 us
  local copies, waits for them, and re-layouts: 29.9 us -> 333 us
  waiting for transfers between devices: 122 us -> 24.4 us
  other arithmetic: 23 us -> 101 us
  starting transfers between devices: 70.1 us -> 9.84 us
  blocking collectives: 80.9 us -> 136 us
    gather x16, local copies, waits for them, and re-layouts: 16 us -> 152 us  [the longest x8 76.1 us: merid_level(): jnp.take(jnp.flip(field_in[:, :rim_depth], axis=1), mirror_map, axis=2)]
    all_to_all x0 -> x8, blocking collectives: none -> 136 us  [exchange(): return lax.all_to_all(parts, AXES, 0, 0, tiled=True)]
    ppermute x40 -> x0, waiting for transfers between devices: 122 us -> none  [the longest x8 56.7 us: from_partner(): lax.ppermute(value, axis, [(i, i ^ 1 << distance) for i in range(lax.axis...]
    rev x0 -> x16, local copies, waits for them, and re-layouts: none -> 102 us  [the longest x8 51.2 us: merid_level(): jnp.flip(field_in[:, :rim_depth], axis=1)]
    psum x2 -> x0, blocking collectives: 80.9 us -> none  [per_device(): lax.psum((jnp.sum(residual * residual), jnp.sum(residual * first), jnp.su...]
    ppermute x40 -> x0, starting transfers between devices: 70.1 us -> none  [the longest x16 52.2 us: extended_2(): lax.ppermute(lax.slice_in_dim(block, block.shape[dim] - width, None, axis...]
    select_n x24 -> x8, other arithmetic: 5.82 us -> 56.8 us  [merid_level(): jnp.take(jnp.flip(field_in[:, :rim_depth], axis=1), mirror_map, axis=2)]
    select_n x0 -> x16, local copies, waits for them, and re-layouts: none -> 30.9 us  [the longest x8 15.7 us: merid_level(): jnp.take(jnp.flip(field_in[:, row_count - rim_depth:], axis=1), mirror_ma...]
  transfers between devices with their start and end apart: 40 -> 2, of which waited for: 26 -> 2; matrix products, arithmetic and copies ran while one was open for 7% -> 0% of each run, Pallas kernels for 0% -> 0%
where the time goes in v1:
time: 662 us; the launch traced here: 650 us
  local copies, waits for them, and re-layouts  333 us (50%)
  blocking collectives  136 us (21%)
  other arithmetic  101 us (15%)
  matrix products  27.7 us (4%)
  waiting for transfers between devices  24.4 us (4%)
  between operations  18 us (3%)
  starting transfers between devices  9.84 us (1%)
    all_to_all x8, blocking collectives, exchange(): return lax.all_to_all(parts, AXES, 0, 0, tiled=True)  136 us
    gather x8, local copies, waits for them, and re-layouts, merid_level(): jnp.take(jnp.flip(field_in[:, :rim_depth], axis=1), mirror_map, axis=2)  76.1 us
    gather x8, local copies, waits for them, and re-layouts, merid_level(): jnp.take(jnp.flip(field_in[:, row_count - rim_depth:], axis=1), mirror_ma...  76 us
    select_n x8, other arithmetic, merid_level(): jnp.take(jnp.flip(field_in[:, :rim_depth], axis=1), mirror_map, axis=2)  56.8 us
    rev x8, local copies, waits for them, and re-layouts, merid_level(): jnp.flip(field_in[:, :rim_depth], axis=1)  51.2 us
    rev x8, local copies, waits for them, and re-layouts, merid_level(): jnp.flip(field_in[:, row_count - rim_depth:], axis=1)  51.1 us
    add x8, other arithmetic, merid_level(): result = result + weights[offset] * (upper + lower)  31.7 us
    unnamed x75, local copies, waits for them, and re-layouts  31.4 us
  transfers between devices with their start and end apart: 2, of which 2 were waited for; matrix products, arithmetic and copies ran while one was open for 0% of the time, Pallas kernels for 0%

profile of v1, /device:TPU:1, one launch (start us, length us, event | category | flops | bytes accessed | tf_op | source)
XLA Modules:
  0.0 649.7 jit_solution(2904484599849216210)
XLA Ops:
  5.5 7.1 %all-to-all-start = ((f32[32,7,4,128]{3,2,1,0:T(4,128)}), f32[32,7,4,128]{3,2,1,0:T(4,128)S(1)}, u32[]{:S(2)}, u32[]{:S(2)}) async-start(f32[32,7,4,128]{3,2,1,0:T(4,128)} %pad_maximum_fusion.19), calls=%async_computation | async-start | bytes 917504 | tf_op jit(solution)/shard_map/all_to_all | solution.py:72
  14.8 11.7 %all-to-all-done = f32[32,7,4,128]{3,2,1,0:T(4,128)S(1)} async-done(((f32[32,7,4,128]{3,2,1,0:T(4,128)}), f32[32,7,4,128]{3,2,1,0:T(4,128)S(1)}, u32[]{:S(2)}, u32[]{:S(2)}) %all-to-all-start) | async-done | bytes 458784 | tf_op jit(solution)/shard_map/all_to_all | solution.py:72
  40.7 6.4 rev.49
  47.1 9.5 %gather_fusion.1 = f32[1024,5,4]{1,2,0:T(4,128)} fusion(f32[5,4,1024]{0,1,2:T(4,128)} %rev.50, s32[1024]{0:T(1024)S(1)} %fusion.246), kind=kCustom, calls=%fused_computation.1.clone | custom fusion | bytes 167936 | tf_op jit(solution)/shard_map/jit(_take)/gather | solution.py:50
  56.6 9.5 %gather_fusion = f32[1024,5,4]{1,2,0:T(4,128)} fusion(f32[5,4,1024]{0,1,2:T(4,128)} %rev.49, s32[1024]{0:T(1024)S(1)} %fusion.246), kind=kCustom, calls=%fused_computation.clone | custom fusion | bytes 167936 | tf_op jit(solution)/shard_map/jit(_take)/gather | solution.py:49
  66.1 7.1 %select_bitcast_fusion.15 = (f32[5,4,1024]{0,1,2:T(4,128)}, f32[5,4,1024]{0,1,2:T(4,128)}) fusion(f32[1024,5,4]{1,2,0:T(4,128)} %gather_fusion, pred[1024]{0:T(1024)(128)(4,1)S(1)} %compare_and_fusion, f32[1024,5,4]{1,2,0:T(4,128)} %gather_fusion.1), kind=kLoop, calls=%fused_computation.33 | loop fusion | flops 40960 | bytes 328704 | tf_op jit(solution)/shard_map/jit(_take)/select_n | solution.py:49
  81.2 14.5 %all_to_all.50 = f32[32,5,4,128]{3,2,1,0:T(4,128)S(1)} all-to-all(f32[32,5,4,128]{3,2,1,0:T(4,128)S(1)} %copy.363), channel_id=1, replica_groups=mesh['lon'=8,'lat'=4] {'lon','lat'}, dimensions={0} | all-to-all | bytes 655360 | tf_op jit(solution)/shard_map/all_to_all | solution.py:72
  96.9 14.3 %all_to_all.51 = f32[32,5,4,128]{3,2,1,0:T(4,128)S(1)} all-to-all(f32[32,5,4,128]{3,2,1,0:T(4,128)S(1)} %bitcast.393), channel_id=1, replica_groups=mesh['lon'=8,'lat'=4] {'lon','lat'}, dimensions={0} | all-to-all | bytes 655360 | tf_op jit(solution)/shard_map/all_to_all | solution.py:72
  113.2 6.4 rev.52
  119.6 9.5 %gather_fusion.3 = f32[1024,5,4]{1,2,0:T(4,128)} fusion(f32[5,4,1024]{0,1,2:T(4,128)} %rev.52, s32[1024]{0:T(1024)S(1)} %fusion.246), kind=kCustom, calls=%fused_computation.3.clone | custom fusion | bytes 167936 | tf_op jit(solution)/shard_map/jit(_take)/gather | solution.py:50
  130.8 6.4 rev.51
  137.2 9.5 %gather_fusion.2 = f32[1024,5,4]{1,2,0:T(4,128)} fusion(f32[5,4,1024]{0,1,2:T(4,128)} %rev.51, s32[1024]{0:T(1024)S(1)} %fusion.246), kind=kCustom, calls=%fused_computation.2.clone | custom fusion | bytes 167936 | tf_op jit(solution)/shard_map/jit(_take)/gather | solution.py:49
  146.8 7.1 %select_bitcast_fusion.13 = (f32[5,4,1024]{0,1,2:T(4,128)}, f32[5,4,1024]{0,1,2:T(4,128)}) fusion(f32[1024,5,4]{1,2,0:T(4,128)} %gather_fusion.2, pred[1024]{0:T(1024)(128)(4,1)S(1)} %compare_and_fusion, f32[1024,5,4]{1,2,0:T(4,128)} %gather_fusion.3), kind=kLoop, calls=%fused_computation.31 | loop fusion | flops 40960 | bytes 328704 | tf_op jit(solution)/shard_map/jit(_take)/select_n | solution.py:49
  170.7 6.4 rev.54
  177.1 9.5 %gather_fusion.5 = f32[1024,5,4]{1,2,0:T(4,128)} fusion(f32[5,4,1024]{0,1,2:T(4,128)} %rev.54, s32[1024]{0:T(1024)S(1)} %fusion.246), kind=kCustom, calls=%fused_computation.5.clone | custom fusion | bytes 167936 | tf_op jit(solution)/shard_map/jit(_take)/gather | solution.py:50
  188.3 6.4 rev.53
  194.7 9.5 %gather_fusion.4 = f32[1024,5,4]{1,2,0:T(4,128)} fusion(f32[5,4,1024]{0,1,2:T(4,128)} %rev.53, s32[1024]{0:T(1024)S(1)} %fusion.246), kind=kCustom, calls=%fused_computation.4.clone | custom fusion | bytes 167936 | tf_op jit(solution)/shard_map/jit(_take)/gather | solution.py:49
  204.2 7.1 %select_bitcast_fusion.11 = (f32[5,4,1024]{0,1,2:T(4,128)}, f32[5,4,1024]{0,1,2:T(4,128)}) fusion(f32[1024,5,4]{1,2,0:T(4,128)} %gather_fusion.4, pred[1024]{0:T(1024)(128)(4,1)S(1)} %compare_and_fusion, f32[1024,5,4]{1,2,0:T(4,128)} %gather_fusion.5), kind=kLoop, calls=%fused_computation.29 | loop fusion | flops 40960 | bytes 328704 | tf_op jit(solution)/shard_map/jit(_take)/select_n | solution.py:49
  219.9 20.6 %all_to_all.52 = f32[32,10,4,128]{3,2,1,0:T(4,128)S(1)} all-to-all(f32[32,10,4,128]{3,2,1,0:T(4,128)S(1)} %copy.387), channel_id=1, replica_groups=mesh['lon'=8,'lat'=4] {'lon','lat'}, dimensions={0} | all-to-all | bytes 1310720 | tf_op jit(solution)/shard_map/all_to_all | solution.py:72
  242.5 14.9 %all_to_all.53 = f32[32,5,4,128]{3,2,1,0:T(4,128)S(1)} all-to-all(f32[32,5,4,128]{3,2,1,0:T(4,128)S(1)} %bitcast.397), channel_id=1, replica_groups=mesh['lon'=8,'lat'=4] {'lon','lat'}, dimensions={0} | all-to-all | bytes 655360 | tf_op jit(solution)/shard_map/all_to_all | solution.py:72
  259.4 6.4 rev.56
  265.8 9.5 %gather_fusion.7 = f32[1024,5,4]{1,2,0:T(4,128)} fusion(f32[5,4,1024]{0,1,2:T(4,128)} %rev.56, s32[1024]{0:T(1024)S(1)} %fusion.246), kind=kCustom, calls=%fused_computation.7.clone | custom fusion | bytes 167936 | tf_op jit(solution)/shard_map/jit(_take)/gather | solution.py:50
  277.1 6.4 rev.55
  283.5 9.5 %gather_fusion.6 = f32[1024,5,4]{1,2,0:T(4,128)} fusion(f32[5,4,1024]{0,1,2:T(4,128)} %rev.55, s32[1024]{0:T(1024)S(1)} %fusion.246), kind=kCustom, calls=%fused_computation.6.clone | custom fusion | bytes 167936 | tf_op jit(solution)/shard_map/jit(_take)/gather | solution.py:49
  293.0 7.1 %select_bitcast_fusion.9 = (f32[5,4,1024]{0,1,2:T(4,128)}, f32[5,4,1024]{0,1,2:T(4,128)}) fusion(f32[1024,5,4]{1,2,0:T(4,128)} %gather_fusion.6, pred[1024]{0:T(1024)(128)(4,1)S(1)} %compare_and_fusion, f32[1024,5,4]{1,2,0:T(4,128)} %gather_fusion.7), kind=kLoop, calls=%fused_computation.27 | loop fusion | flops 40960 | bytes 328704 | tf_op jit(solution)/shard_map/jit(_take)/select_n | solution.py:49
  316.9 6.4 rev.58
  323.3 9.5 %gather_fusion.9 = f32[1024,5,4]{1,2,0:T(4,128)} fusion(f32[5,4,1024]{0,1,2:T(4,128)} %rev.58, s32[1024]{0:T(1024)S(1)} %fusion.246), kind=kCustom, calls=%fused_computation.9.clone | custom fusion | bytes 167936 | tf_op jit(solution)/shard_map/jit(_take)/gather | solution.py:50
  334.6 6.4 rev.57
  341.0 9.5 %gather_fusion.8 = f32[1024,5,4]{1,2,0:T(4,128)} fusion(f32[5,4,1024]{0,1,2:T(4,128)} %rev.57, s32[1024]{0:T(1024)S(1)} %fusion.246), kind=kCustom, calls=%fused_computation.8.clone | custom fusion | bytes 167936 | tf_op jit(solution)/shard_map/jit(_take)/gather | solution.py:49
  350.5 7.1 %select_bitcast_fusion.7 = (f32[5,4,1024]{0,1,2:T(4,128)}, f32[5,4,1024]{0,1,2:T(4,128)}) fusion(f32[1024,5,4]{1,2,0:T(4,128)} %gather_fusion.8, pred[1024]{0:T(1024)(128)(4,1)S(1)} %compare_and_fusion, f32[1024,5,4]{1,2,0:T(4,128)} %gather_fusion.9), kind=kLoop, calls=%fused_computation.25 | loop fusion | flops 40960 | bytes 328704 | tf_op jit(solution)/shard_map/jit(_take)/select_n | solution.py:49
  372.6 22.0 %all_to_all.54 = f32[32,11,4,128]{3,2,1,0:T(4,128)S(1)} all-to-all(f32[32,11,4,128]{3,2,1,0:T(4,128)S(1)} %copy.411), channel_id=1, replica_groups=mesh['lon'=8,'lat'=4] {'lon','lat'}, dimensions={0} | all-to-all | bytes 1441792 | tf_op jit(solution)/shard_map/all_to_all | solution.py:72
  405.1 14.5 %all_to_all.55 = f32[32,5,4,128]{3,2,1,0:T(4,128)S(1)} all-to-all(f32[32,5,4,128]{3,2,1,0:T(4,128)S(1)} %bitcast.401), channel_id=1, replica_groups=mesh['lon'=8,'lat'=4] {'lon','lat'}, dimensions={0} | all-to-all | bytes 655360 | tf_op jit(solution)/shard_map/all_to_all | solution.py:72
  423.3 6.4 rev.60
  429.7 9.5 %gather_fusion.11 = f32[1024,5,4]{1,2,0:T(4,128)} fusion(f32[5,4,1024]{0,1,2:T(4,128)} %rev.60, s32[1024]{0:T(1024)S(1)} %fusion.246), kind=kCustom, calls=%fused_computation.11.clone | custom fusion | bytes 167936 | tf_op jit(solution)/shard_map/jit(_take)/gather | solution.py:50
  440.9 6.4 rev.59
  447.3 9.5 %gather_fusion.10 = f32[1024,5,4]{1,2,0:T(4,128)} fusion(f32[5,4,1024]{0,1,2:T(4,128)} %rev.59, s32[1024]{0:T(1024)S(1)} %fusion.246), kind=kCustom, calls=%fused_computation.10.clone | custom fusion | bytes 167936 | tf_op jit(solution)/shard_map/jit(_take)/gather | solution.py:49
  456.9 7.1 %select_bitcast_fusion.5 = (f32[5,4,1024]{0,1,2:T(4,128)}, f32[5,4,1024]{0,1,2:T(4,128)}) fusion(f32[1024,5,4]{1,2,0:T(4,128)} %gather_fusion.10, pred[1024]{0:T(1024)(128)(4,1)S(1)} %compare_and_fusion, f32[1024,5,4]{1,2,0:T(4,128)} %gather_fusion.11), kind=kLoop, calls=%fused_computation.23 | loop fusion | flops 40960 | bytes 328704 | tf_op jit(solution)/shard_map/jit(_take)/select_n | solution.py:49
  485.6 9.5 %gather_fusion.13 = f32[1024,5,4]{1,2,0:T(4,128)} fusion(f32[5,4,1024]{0,1,2:T(4,128)} %rev.62, s32[1024]{0:T(1024)S(1)} %fusion.246), kind=kCustom, calls=%fused_computation.13.clone | custom fusion | bytes 167936 | tf_op jit(solution)/shard_map/jit(_take)/gather | solution.py:50
  496.8 6.4 rev.61
  503.2 9.5 %gather_fusion.12 = f32[1024,5,4]{1,2,0:T(4,128)} fusion(f32[5,4,1024]{0,1,2:T(4,128)} %rev.61, s32[1024]{0:T(1024)S(1)} %fusion.246), kind=kCustom, calls=%fused_computation.12.clone | custom fusion | bytes 167936 | tf_op jit(solution)/shard_map/jit(_take)/gather | solution.py:49
  512.7 7.1 %select_bitcast_fusion.3 = (f32[5,4,1024]{0,1,2:T(4,128)}, f32[5,4,1024]{0,1,2:T(4,128)}) fusion(f32[1024,5,4]{1,2,0:T(4,128)} %gather_fusion.12, pred[1024]{0:T(1024)(128)(4,1)S(1)} %compare_and_fusion, f32[1024,5,4]{1,2,0:T(4,128)} %gather_fusion.13), kind=kLoop, calls=%fused_computation.21 | loop fusion | flops 40960 | bytes 328704 | tf_op jit(solution)/shard_map/jit(_take)/select_n | solution.py:49
  529.5 20.6 %all_to_all.56 = f32[32,10,4,128]{3,2,1,0:T(4,128)S(1)} all-to-all(f32[32,10,4,128]{3,2,1,0:T(4,128)S(1)} %copy.437), channel_id=1, replica_groups=mesh['lon'=8,'lat'=4] {'lon','lat'}, dimensions={0} | all-to-all | bytes 1310720 | tf_op jit(solution)/shard_map/all_to_all | solution.py:72
  552.1 14.5 %all_to_all.57 = f32[32,5,4,128]{3,2,1,0:T(4,128)S(1)} all-to-all(f32[32,5,4,128]{3,2,1,0:T(4,128)S(1)} %bitcast.390), channel_id=1, replica_groups=mesh['lon'=8,'lat'=4] {'lon','lat'}, dimensions={0} | all-to-all | bytes 655360 | tf_op jit(solution)/shard_map/all_to_all | solution.py:72
  568.6 6.4 rev.64
  575.0 9.5 %gather_fusion.15 = f32[1024,5,4]{1,2,0:T(4,128)} fusion(f32[5,4,1024]{0,1,2:T(4,128)} %rev.64, s32[1024]{0:T(1024)S(1)} %fusion.246), kind=kCustom, calls=%fused_computation.15.clone | custom fusion | bytes 167936 | tf_op jit(solution)/shard_map/jit(_take)/gather | solution.py:50
  592.6 9.5 %gather_fusion.14 = f32[1024,5,4]{1,2,0:T(4,128)} fusion(f32[5,4,1024]{0,1,2:T(4,128)} %rev.63, s32[1024]{0:T(1024)S(1)} %fusion.246), kind=kCustom, calls=%fused_computation.14.clone | custom fusion | bytes 167936 | tf_op jit(solution)/shard_map/jit(_take)/gather | solution.py:49
  602.2 7.1 %select_bitcast_fusion.1 = (f32[5,4,1024]{0,1,2:T(4,128)}, f32[5,4,1024]{0,1,2:T(4,128)}) fusion(f32[1024,5,4]{1,2,0:T(4,128)} %gather_fusion.14, pred[1024]{0:T(1024)(128)(4,1)S(1)} %compare_and_fusion, f32[1024,5,4]{1,2,0:T(4,128)} %gather_fusion.15), kind=kLoop, calls=%fused_computation.19 | loop fusion | flops 40960 | bytes 328704 | tf_op jit(solution)/shard_map/jit(_take)/select_n | solution.py:49
  626.7 12.6 %all-to-all-done.9 = f32[32,6,4,128]{3,2,1,0:T(4,128)S(1)} async-done(((f32[32,6,4,128]{3,2,1,0:T(4,128)}), f32[32,6,4,128]{3,2,1,0:T(4,128)S(1)}, u32[]{:S(2)}, u32[]{:S(2)}) %all-to-all-start.9) | async-done | bytes 393248 | tf_op jit(solution)/shard_map/all_to_all | solution.py:72
  (226 shorter events, 172.1 us)
Async XLA Ops:
  0.6 95.1 %copy-start = (f32[137,137]{1,0:T(8,128)S(1)}, f32[137,137]{1,0:T(8,128)}, u32[]{:S(2)}) copy-start(f32[137,137]{1,0:T(8,128)} %param.23) | copy-start | bytes 225232
  0.6 12.0 %copy-start.21 = (f32[5]{0:T(128)S(1)}, f32[5]{0:T(128)}, u32[]{:S(2)}) copy-start(f32[5]{0:T(128)} %param.22) | copy-start | bytes 64
  5.5 21.0 %all-to-all-start = ((f32[32,7,4,128]{3,2,1,0:T(4,128)}), f32[32,7,4,128]{3,2,1,0:T(4,128)S(1)}, u32[]{:S(2)}, u32[]{:S(2)}) async-start(f32[32,7,4,128]{3,2,1,0:T(4,128)} %pad_maximum_fusion.19), calls=%async_computation | async-start | bytes 917504 | tf_op jit(solution)/shard_map/all_to_all | solution.py:72
  77.0 18.7 %copy-start.4 = (f32[137,4,128]{2,1,0:T(4,128)S(1)}, f32[137,4,128]{2,1,0:T(4,128)}, u32[]{:S(2)}) copy-start(f32[137,4,128]{2,1,0:T(4,128)} %param.18) | copy-start | bytes 841732
  95.7 15.6 %copy-start.9 = (f32[137,4,128]{2,1,0:T(4,128)}, f32[137,4,128]{2,1,0:T(4,128)S(1)}, u32[]{:S(2)}) copy-start(f32[137,4,128]{2,1,0:T(4,128)S(1)} %slice.900) | copy-start | bytes 841732
  215.2 3.9 copy-start.16
  219.4 21.9 %copy-start.1 = (f32[5,4,4,8,128]{4,1,3,2,0:T(4,128)}, f32[5,4,4,8,128]{4,1,3,2,0:T(4,128)S(1)}, u32[]{:S(2)}) copy-start(f32[5,4,4,8,128]{4,1,3,2,0:T(4,128)S(1)} %bitcast_add_fusion.3) | copy-start | bytes 983044
  241.3 16.3 %copy-start.11 = (f32[137,4,128]{2,1,0:T(4,128)}, f32[137,4,128]{2,1,0:T(4,128)S(1)}, u32[]{:S(2)}) copy-start(f32[137,4,128]{2,1,0:T(4,128)S(1)} %slice.938) | copy-start | bytes 841732
  315.1 8.2 %copy-start.13 = (f32[5,16,1024]{2,1,0:T(8,128)}, f32[5,16,1024]{2,1,0:T(8,128)S(1)}, u32[]{:S(2)}) copy-start(f32[5,16,1024]{2,1,0:T(8,128)S(1)} %reshape.393) | copy-start | bytes 983044
  359.5 8.8 %copy-start.2 = (f32[5,4,4,8,128]{4,1,3,2,0:T(4,128)S(1)}, f32[5,4,4,8,128]{4,1,3,2,0:T(4,128)}, u32[]{:S(2)}) copy-start(f32[5,4,4,8,128]{4,1,3,2,0:T(4,128)} %copy-done.1) | copy-start | bytes 983044
  361.6 6.7 %copy-start.15 = (f32[16,128,5,8]{1,3,2,0:T(8,128)S(1)}, f32[16,128,5,8]{1,3,2,0:T(8,128)}, u32[]{:S(2)}) copy-start(f32[16,128,5,8]{1,3,2,0:T(8,128)} %get-tuple-element.155) | copy-start | bytes 983044
  369.5 25.1 %copy-start.7 = (f32[5,4,4,8,128]{4,1,3,2,0:T(4,128)}, f32[5,4,4,8,128]{4,1,3,2,0:T(4,128)S(1)}, u32[]{:S(2)}) copy-start(f32[5,4,4,8,128]{4,1,3,2,0:T(4,128)S(1)} %get-tuple-element.66) | copy-start | bytes 983044
  372.1 31.7 %copy-start.5 = (f32[137,4,128]{2,1,0:T(4,128)S(1)}, f32[137,4,128]{2,1,0:T(4,128)}, u32[]{:S(2)}) copy-start(f32[137,4,128]{2,1,0:T(4,128)} %param.18) | copy-start | bytes 841732
  372.1 31.7 %copy-start.10 = (f32[137,4,128]{2,1,0:T(4,128)S(1)}, f32[137,4,128]{2,1,0:T(4,128)}, u32[]{:S(2)}) copy-start(f32[137,4,128]{2,1,0:T(4,128)} %copy-done.9) | copy-start | bytes 841732
  372.1 31.7 %copy-start.12 = (f32[137,4,128]{2,1,0:T(4,128)S(1)}, f32[137,4,128]{2,1,0:T(4,128)}, u32[]{:S(2)}) copy-start(f32[137,4,128]{2,1,0:T(4,128)} %copy-done.11) | copy-start | bytes 841732
  521.7 6.2 copy-start.3
  521.7 6.2 copy-start.8
  523.9 4.0 copy-start.14
  529.0 21.9 %copy-start.6 = (f32[137,4,128]{2,1,0:T(4,128)S(1)}, f32[137,4,128]{2,1,0:T(4,128)}, u32[]{:S(2)}) copy-start(f32[137,4,128]{2,1,0:T(4,128)} %param.18) | copy-start | bytes 841732
  619.9 6.7 %copy-start.17 = (f32[32,5,4,128]{3,2,1,0:T(4,128)S(1)}, f32[32,5,4,128]{3,2,1,0:T(4,128)}, u32[]{:S(2)}) copy-start(f32[32,5,4,128]{3,2,1,0:T(4,128)} %get-tuple-element.73) | copy-start | bytes 983044
  619.9 6.8 %copy-start.18 = (f32[32,5,4,128]{3,2,1,0:T(4,128)S(1)}, f32[32,5,4,128]{3,2,1,0:T(4,128)}, u32[]{:S(2)}) copy-start(f32[32,5,4,128]{3,2,1,0:T(4,128)} %get-tuple-element.69) | copy-start | bytes 983044
  619.9 6.8 %copy-start.19 = (f32[32,5,4,128]{3,2,1,0:T(4,128)S(1)}, f32[32,5,4,128]{3,2,1,0:T(4,128)}, u32[]{:S(2)}) copy-start(f32[32,5,4,128]{3,2,1,0:T(4,128)} %get-tuple-element.72) | copy-start | bytes 983044
  622.9 24.8 %copy-start.20 = (f32[137,4,128]{2,1,0:T(4,128)S(1)}, f32[137,4,128]{2,1,0:T(4,128)}, u32[]{:S(2)}) copy-start(f32[137,4,128]{2,1,0:T(4,128)} %param.17) | copy-start | bytes 841732
  623.9 15.5 %all-to-all-start.9 = ((f32[32,6,4,128]{3,2,1,0:T(4,128)}), f32[32,6,4,128]{3,2,1,0:T(4,128)S(1)}, u32[]{:S(2)}, u32[]{:S(2)}) async-start(f32[32,6,4,128]{3,2,1,0:T(4,128)} %copy.454), calls=%async_computation.9 | async-start | bytes 786432 | tf_op jit(solution)/shard_map/all_to_all | solution.py:72
